TPU v7x, 512 devices: a whole 4x8x8 slice. The times are simulated.
512 devices in a mesh: comp: 2 (over x_lo), tile: 128 (over z, x_hi, y), lev: 2 (over core).
Axes of the slice: x: 4 (x_hi: 2, x_lo: 2; x = x_hi * 2 + x_lo), y: 8, z: 8, core: 2. Of those that a mesh axis runs over, the one named last changes fastest.
Arguments:
- adj_final: float32 [2, 72, 32768], P('comp', 'lev', 'tile'), may hold values from -6 to 6
- flipped_vertical_steppers: float32 [2, 72, 72], P('comp', 'lev'), as said below
- profiles: float32 [2, 6, 72], P('comp', None, 'lev'), may hold values from -0.9 to 0.9
- skin_sensitivity_pair: float32 [2, 72], P('comp', 'lev'), may hold values from -0.9 to 0.9
- match: int32 [128], replicated, may hold values from 0 to 127, each once
- remap_offs: int32 [256, 4], P('tile'), may hold values from 0 to 5
- remap_count: int32 [256], P('tile'), may hold values from 1 to 4, as said below
- conserving_transfer_factors: float32 [256, 4, 128, 128], P('tile'), may hold values from -0.25 to 0.25
Outputs:
- adj_initial: float32 [2, 72, 32768], P('comp', 'lev', 'tile')
Inputs may be any that keep to these rules, and one draw needn't show every extreme that they name: `match`: the atmosphere tiles in some order, each once. `remap_offs`: entries at or past a row block's count are to be ignored. `remap_count`: some row block uses all 4 entries. `flipped_vertical_steppers`: off-diagonal entries weigh about as much as the diagonal in each row.
All inputs are finite; a program needn't handle non-finite values.
Results may differ from a plain program's by a relative error of at most 0.00014.
Values sent between devices are 32-bit elements; how exact they have to be, the bound alone decides.
A program may use at most 64 MiB of HBM per device.

v0:
```python
import jax
import jax.numpy as jnp
from jax import lax
from jax.sharding import PartitionSpec as P

STEPS = 6
NBMAX = 4
HIGH_ACCURACY = lax.Precision.HIGHEST


def passed_along(block, axis, distance):
    devices = range(lax.axis_size(axis))
    route = [(i - distance, i) for i in devices if i - distance in devices]
    return lax.ppermute(block, axis, route)


def hit_rows(target, count):
    spots = lax.broadcasted_iota(jnp.int32, (count, target.shape[0]), 0)
    return (spots == target[None, :]).astype(jnp.float32)


def level_adder(operator):

    def add_piece(total, piece, start):
        return jnp.dot(operator, piece, precision=HIGH_ACCURACY, preferred_element_type=jnp.float32)

    return add_piece


def on_device(
    adj_final,
    flipped_vertical_steppers,
    profiles,
    skin_sensitivity_pair,
    match,
    remap_offs,
    remap_count,
    conserving_transfer_factors,
):
    tile_blocks = remap_offs.shape[0]
    block = conserving_transfer_factors.shape[2]
    grid_cells = adj_final.shape[2]
    tiles = lax.axis_size("tile")
    blocks = tiles * tile_blocks
    entries = tile_blocks * NBMAX
    own_state = adj_final[0]
    operator = flipped_vertical_steppers[0]
    flux_rows = profiles[0]
    skin_factor_vector = skin_sensitivity_pair[0]
    add_levels = level_adder(operator)
    first_block = (match[lax.axis_index("tile")] - 1) * tile_blocks
    target = jnp.mod(first_block + remap_offs, blocks).reshape(entries)
    in_use = (
        lax.broadcasted_iota(jnp.int32, (tile_blocks, NBMAX), 1) < remap_count[:, None]
    ).astype(jnp.float32)
    partial_flux = jnp.dot(flux_rows, own_state, precision=HIGH_ACCURACY)
    phi_ocn = lax.psum(partial_flux, "lev")
    phi_rows = phi_ocn.reshape(STEPS, tile_blocks, block).transpose(1, 0, 2)
    contrib = (
        jnp.einsum("reij,rsi->resj", conserving_transfer_factors, phi_rows, precision=HIGH_ACCURACY)
        * in_use[:, :, None, None]
    )
    flat = contrib.reshape(entries, STEPS * block)
    mine = lax.psum_scatter(
        jnp.dot(
            hit_rows(target, tile_blocks * lax.axis_size("tile")), flat, precision=HIGH_ACCURACY
        ),
        "tile",
        scatter_dimension=0,
        tiled=True,
    )
    flux_atm = mine.reshape(tile_blocks, STEPS, block).transpose(1, 0, 2).reshape(STEPS, grid_cells)
    flux_atm = passed_along(flux_atm, "comp", -1)
    adjoint = own_state
    surface_part = jnp.zeros((grid_cells,), jnp.float32)
    for step in reversed(range(STEPS)):
        flux_now = flux_atm[step]
        adjoint = adjoint + flux_rows[step][:, None] * flux_now[None, :]
        surface_part = surface_part + jnp.dot(skin_factor_vector, adjoint, precision=HIGH_ACCURACY)
        adjoint = add_levels(
            jnp.zeros_like(adjoint),
            lax.all_gather(adjoint, "lev", axis=0, tiled=True),
            jnp.int32(0),
        )
    marine_share = add_levels(
        jnp.zeros_like(own_state),
        lax.all_gather(own_state, "lev", axis=0, tiled=True),
        jnp.int32(0),
    )
    surface_adj = lax.psum(surface_part, "lev")
    surface_adj = passed_along(surface_adj, "comp", 1)
    piece = lax.all_gather(surface_adj.reshape(tile_blocks, block), "tile", axis=0, tiled=True)
    hits = (
        target[:, None] == lax.broadcasted_iota(jnp.int32, (entries, piece.shape[0]), 1)
    ).astype(jnp.float32)
    chosen_tile_matrices = jnp.dot(hits, piece, precision=HIGH_ACCURACY)
    chosen_tile_matrices = (
        chosen_tile_matrices.reshape(tile_blocks, NBMAX, block) * in_use[:, :, None]
    )
    marine_skin_warmth = jnp.einsum(
        "dcfv,dcv->df", conserving_transfer_factors, chosen_tile_matrices, precision=HIGH_ACCURACY
    ).reshape(grid_cells)
    marine_tile_matrix = marine_share + skin_factor_vector[:, None] * marine_skin_warmth[None, :]
    is_atmos = lax.axis_index("comp") == 0
    return jnp.where(is_atmos, adjoint, marine_tile_matrix)[None]


def solution(mesh):
    return jax.shard_map(
        on_device,
        mesh=mesh,
        in_specs=(
            P("comp", "lev", "tile"),
            P("comp", "lev", None),
            P("comp", None, "lev"),
            P("comp", "lev"),
            P(),
            P("tile", None),
            P("tile"),
            P("tile", None, None, None),
        ),
        out_specs=P("comp", "lev", "tile"),
        check_vma=False,
    )
```

profile of v0, /device:TPU:2, one launch (start us, length us, event | category | flops | bytes accessed | tf_op | source)
XLA Modules:
  0.0 1725.5 jit_solution(2810413761851644490)
XLA Ops:
  6.5 0.0 copy-start
  6.5 0.0 all-reduce.3.cloned.1.call-start
  6.5 0.0 copy-start.6
  6.5 0.7 copy-done.6
  7.3 0.6 dynamic_slice.3
  8.5 0.0 copy-start.5
  8.5 0.7 copy-done.5
  9.2 0.0 copy-start.7
  9.2 0.1 eq.24
  9.3 0.6 copy-done.7
  9.8 0.1 compare_convert_fusion
  9.9 0.0 copy-done.3
  9.9 0.9 convolution_bitcast_fusion.6
  10.8 2.5 psum.14
  13.3 0.0 copy-done
  13.3 0.4 convolution_multiply_fusion
  13.7 1.3 fusion.2
  15.0 0.0 all-reduce.3.cloned.1.call-update
  15.0 0.0 copy-start.2
  15.0 1.3 dynamic-slice
  17.0 1322.4 %all-reduce.3.cloned.1.call-done = f32[256,768]{1,0:T(8,128)} async-done(((f32[256,768]{1,0:T(8,128)}), f32[256,768]{1,0:T(8,128)}) %all-reduce.3.cloned.1.call-update) | async-done | bytes 786448
  1339.4 0.7 constant_dynamic-slice_fusion
  1340.2 3.4 collective-permute-start
  1343.5 0.0 copy-done.2
  1343.5 1.9 all-gather
  1345.4 0.0 collective-permute-done
  1345.4 0.1 fusion.10
  1345.5 1.9 all-gather.1
  1347.3 0.0 copy-start.1
  1347.3 0.7 copy-done.1
  1348.1 0.2 convolution_bitcast_fusion.5
  1348.2 0.1 fusion.13
  1348.3 1.9 all-gather.2
  1350.2 0.2 convolution_bitcast_fusion.4
  1350.4 0.1 fusion.15
  1350.4 1.9 all-gather.3
  1352.3 0.2 convolution_bitcast_fusion.3
  1352.5 0.1 fusion.17
  1352.6 1.9 all-gather.4
  1354.4 0.2 convolution_bitcast_fusion.2
  1354.6 0.0 copy-start.4
  1354.6 0.1 fusion.19
  1354.7 0.6 copy-done.4
  1355.3 0.2 fusion.18
  1355.5 0.2 fusion.16
  1355.7 0.2 fusion.14
  1355.9 0.2 fusion.12
  1356.1 0.1 multiply_add_fusion.5
  1356.2 1.9 all-gather.5
  1358.1 0.2 convolution_bitcast_fusion.1
  1358.3 0.2 fusion.20
  1358.5 0.1 fusion.21
  1358.6 0.1 fusion.6
  1358.8 2.5 psum.15
  1361.2 1.3 collective-permute-start.1
  1362.5 1.9 all-gather.6
  1364.4 0.2 convolution_bitcast_fusion
  1364.6 2.1 collective-permute-done.1
  1366.7 350.3 %all-gather.7 = f32[128,2,128]{2,1,0:T(2,128)S(1)} all-gather(f32[1,2,128]{2,1,0:T(2,128)S(1)} %bitcast.160), channel_id=1, replica_groups=mesh['comp'=2,'tile'=128,'lev'=2] {'tile'}, dimensions={0}, use_global_device_ids=true | all-gather | bytes 132096 | tf_op jit(solution)/shard_map/all_gather | solution.py:92
  1717.0 0.2 fusion.49
  1717.2 0.1 broadcast_multiply_fusion
  1717.2 0.5 fusion.61
  1717.8 0.2 fusion.1
  1718.0 0.7 copy.14
  (12 shorter events, 0.1 us)
Async XLA Ops:
  6.5 6.8 copy-start
  6.5 1332.9 %all-reduce.3.cloned.1.call-start = ((), (), s32[]{:S(2)}) async-start(), calls=%async_computation | async-start | bytes 1572864
  6.5 0.7 copy-start.6
  8.5 0.7 copy-start.5
  9.2 0.7 copy-start.3
  9.2 0.7 copy-start.7
  15.0 1328.5 %copy-start.2 = (f32[1,36,256]{2,0,1:T(1,128)S(1)}, f32[1,36,256]{2,0,1:T(1,128)}, u32[]{:S(2)}) copy-start(f32[1,36,256]{2,0,1:T(1,128)} %param.8) | copy-start | bytes 110596
  1340.2 5.2 collective-permute-start
  1347.3 0.7 copy-start.1
  1354.6 0.7 copy-start.4
  1361.2 5.5 collective-permute-start.1
Sparse Core Ops, SparseCore 0:
  15.2 1324.1 all-reduce.2
where the time goes:
time: 1730 us
  waiting for transfers between devices  1320 us (76%)
  blocking collectives  368 us (21%)
    unnamed x2, waiting for transfers between devices  1320 us
    all_gather x1, blocking collectives, on_device(): lax.all_gather(surface_adj.reshape(tile_blocks, block), 'tile', axis=0, t...  350 us
  transfers between devices with their start and end apart: 3, of which 2 were waited for; matrix products, arithmetic and copies ran while one was open for 0% of the time, Pallas kernels for 0%

commit v1 on v0

--- a/solution.py
+++ b/solution.py
@@ -89,7 +89,11 @@
     )
     surface_adj = lax.psum(surface_part, "lev")
     surface_adj = passed_along(surface_adj, "comp", 1)
-    piece = lax.all_gather(surface_adj.reshape(tile_blocks, block), "tile", axis=0, tiled=True)
+    x = surface_adj.reshape(tile_blocks, block)
+    size = lax.axis_size("tile")
+    parts = jnp.stack([x for _ in range(size)])
+    parts = lax.all_to_all(parts, "tile", split_axis=0, concat_axis=0)
+    piece = jnp.concatenate(parts, axis=0)
     hits = (
         target[:, None] == lax.broadcasted_iota(jnp.int32, (entries, piece.shape[0]), 1)
     ).astype(jnp.float32)

time: 1730 us -> 1400 us (0.81)
  the two profiles are of different devices: /device:TPU:2 before, /device:TPU:1 now
where the time goes in v1:
time: 1400 us
  waiting for transfers between devices  1260 us (90%)
  blocking collectives  98.7 us (7%)
  between operations  14.9 us (1%)
    unnamed x2, waiting for transfers between devices  1250 us
    all_gather x6, blocking collectives, on_device(): lax.all_gather(adjoint, 'lev', axis=0, tiled=True)  85.1 us
  transfers between devices with their start and end apart: 4, of which 3 were waited for; matrix products, arithmetic and copies ran while one was open for 0% of the time, Pallas kernels for 0%

profile of v1, /device:TPU:1, one launch (start us, length us, event | category | flops | bytes accessed | tf_op | source)
XLA Modules:
  0.0 1399.1 jit_solution(14343513649921902517)
XLA Ops:
  6.5 0.0 copy-start
  6.5 0.0 all-reduce.3.cloned.1.call-start
  6.5 0.0 copy-start.6
  6.5 0.7 copy-done.6
  7.3 0.6 dynamic_slice.3
  8.5 0.0 copy-start.5
  8.5 0.7 copy-done.5
  9.2 0.0 copy-start.7
  9.2 0.1 eq.40
  9.3 0.6 copy-done.7
  9.8 0.1 compare_convert_fusion
  9.9 0.0 copy-done.3
  9.9 0.9 convolution_bitcast_fusion.6
  10.8 9.0 psum.14
  19.8 0.0 copy-done
  19.8 0.4 convolution_multiply_fusion
  20.2 1.4 fusion.2
  21.6 0.0 all-reduce.3.cloned.1.call-update
  21.6 0.0 copy-start.2
  21.6 1.3 dynamic-slice
  23.5 1245.0 %all-reduce.3.cloned.1.call-done = f32[256,768]{1,0:T(8,128)} async-done(((f32[256,768]{1,0:T(8,128)}), f32[256,768]{1,0:T(8,128)}) %all-reduce.3.cloned.1.call-update) | async-done | bytes 786448
  1268.6 0.7 constant_dynamic-slice_fusion
  1269.3 1.3 collective-permute-start
  1270.6 3.5 collective-permute-done
  1274.1 0.0 copy-done.2
  1274.1 0.1 fusion.10
  1274.2 75.5 %all-gather.1 = f32[2,36,256]{2,1,0:T(8,128)S(1)} all-gather(f32[1,36,256]{2,1,0:T(8,128)S(1)} %fusion.10), channel_id=1, replica_groups=mesh['comp'=2,'tile'=128,'lev'=2] {'lev'}, dimensions={0}, use_global_device_ids=true | all-gather | bytes 110592 | tf_op jit(solution)/shard_map/all_gather | solution.py:82
  1349.7 0.7 copy-done.1
  1350.5 0.2 convolution_bitcast_fusion.5
  1350.6 0.1 fusion.13
  1350.7 1.9 all-gather.2
  1352.6 0.2 convolution_bitcast_fusion.4
  1352.8 0.1 fusion.15
  1352.8 1.9 all-gather.3
  1354.7 0.2 convolution_bitcast_fusion.3
  1354.9 0.1 fusion.17
  1355.0 1.9 all-gather.4
  1356.8 0.2 convolution_bitcast_fusion.2
  1357.0 0.0 copy-start.4
  1357.0 0.1 fusion.19
  1357.1 0.6 copy-done.4
  1357.7 0.2 fusion.18
  1357.9 0.2 fusion.16
  1358.1 0.2 fusion.14
  1358.3 0.2 fusion.12
  1358.5 0.1 multiply_add_fusion.5
  1358.6 1.9 all-gather.5
  1360.5 0.2 convolution_bitcast_fusion.1
  1360.7 0.1 fusion.6
  1360.8 0.2 fusion.20
  1361.1 2.5 psum.15
  1363.5 1.4 collective-permute-start.1
  1364.9 2.1 all-gather
  1367.0 0.0 collective-permute-done.1
  1367.0 0.7 stack.3
  1367.7 9.6 all-to-all-start
  1377.3 0.1 fusion.21
  1377.4 2.1 all-gather.6
  1379.5 0.2 convolution_bitcast_fusion
  1379.7 10.9 all-to-all-done
  1390.7 0.2 convolution_multiply_fusion.1
  1390.9 0.5 fusion.62
  1391.4 0.2 fusion.1
  1391.6 0.7 copy.14
  (13 shorter events, 0.1 us)
Async XLA Ops:
  6.5 13.3 copy-start
  6.5 1262.0 %all-reduce.3.cloned.1.call-start = ((), (), s32[]{:S(2)}) async-start(), calls=%async_computation.1 | async-start | bytes 1572864
  6.5 0.7 copy-start.6
  8.5 0.7 copy-start.5
  9.2 0.7 copy-start.3
  9.2 0.7 copy-start.7
  21.6 1252.5 %copy-start.2 = (f32[1,36,256]{2,0,1:T(1,128)S(1)}, f32[1,36,256]{2,0,1:T(1,128)}, u32[]{:S(2)}) copy-start(f32[1,36,256]{2,0,1:T(1,128)} %param.8) | copy-start | bytes 110596
  1269.3 4.8 collective-permute-start
  1349.7 0.7 copy-start.1
  1357.0 0.7 copy-start.4
  1363.5 3.5 collective-permute-start.1
  1367.7 22.9 %all-to-all-start = ((f32[128,2,128]{2,1,0:T(2,128)}), f32[128,2,128]{2,1,0:T(2,128)S(1)}, u32[]{:S(2)}, u32[]{:S(2)}) async-start(f32[128,2,128]{2,1,0:T(2,128)} %stack.3), calls=%async_computation | async-start | bytes 262144 | tf_op jit(solution)/shard_map/all_to_all | solution.py:95
Sparse Core Ops, SparseCore 0:
  21.7 1246.8 all-reduce.2
